TPU v7x, 32 devices: a whole 2x2x4 slice. The times are simulated.
32 devices in a mesh: tm: 4 (over y, core), dom: 8 (over z, x).
Axes of the slice: x: 2, y: 2, z: 4, core: 2. Of those that a mesh axis runs over, the one named last changes fastest.
Arguments:
- particles: float32 [4, 64, 4096], P('tm', None, 'dom'), may hold values from -12 to 12, as said below
- noise: float32 [4, 64, 4096], P('tm', None, 'dom'), may hold values from -6 to 6
Outputs:
- advanced: float32 [4, 64, 4096], P('tm', None, 'dom')
Inputs may be any that keep to these rules, and one draw needn't show every extreme that they name: `particles`: positions of cells in principal components, each time point about a shifted centre.
All inputs are finite; a program needn't handle non-finite values.
Results may differ from a plain program's by a relative error of at most 0.012.
The roundings to bfloat16 on the way count: a program that leaves them out, or rounds other values in their place, can miss the bound.
Values may be sent and summed in bfloat16 or wider, within the bound.
A program may use at most 64 MiB of HBM per device.

v0:
```python
import math

import jax
import jax.numpy as jnp
from jax import lax
from jax.sharding import PartitionSpec as P

SWEEPS = 2


EPS = 4.0
STEP = 0.5
TEMP = 0.05


def passed_along(value, axis, steps):
    count = lax.axis_size(axis)
    leading, last = (max(0, -steps), min(count, count - steps))
    return lax.ppermute(value, axis, [(source, source + steps) for source in range(leading, last)])


def col_tiles(targets, potential):
    features = targets.shape[0]
    col_count = targets.shape[1]
    tile_width = math.gcd(col_count, 1024)
    tile_count = col_count // tile_width
    tiles = targets.reshape(features, tile_count, tile_width).transpose(1, 0, 2)
    return (tiles, potential.reshape(tile_count, tile_width))


def tile_scores(sources, target_tile, pot_tile):
    products = lax.dot_general(
        sources, target_tile, (((0,), (0,)), ((), ())), preferred_element_type=jnp.float32
    )
    return (products + pot_tile[None, :]) / EPS


def log_totals(sources, tiles, pot_tiles):
    row_count = sources.shape[1]

    def log_advance(carry, pieces):
        highest, totals = carry
        scores = tile_scores(sources, pieces[0], pieces[1])
        merged = jnp.maximum(highest, jnp.max(scores, axis=1))
        totals = totals * jnp.exp(highest - merged) + jnp.sum(
            jnp.exp(scores - merged[:, None]), axis=1
        )
        return ((merged, totals), None)

    start = (jnp.full((row_count,), -jnp.inf, jnp.float32), jnp.zeros((row_count,), jnp.float32))
    (highest, totals), unused = lax.scan(log_advance, start, (tiles, pot_tiles))
    return (highest, totals)


def update(sources, targets, potential):
    tiles, pot_tiles = col_tiles(targets, potential)
    highest, totals = log_totals(sources, tiles, pot_tiles)
    result = -EPS * (highest + jnp.log(totals)) + EPS * math.log(targets.shape[1])
    return (result, highest, totals)


def barycentre(sources, targets, potential, highest, totals):
    tiles, pot_tiles = col_tiles(targets, potential)

    def barycentre_advance(summed, pieces):
        scores = tile_scores(sources, pieces[0], pieces[1])
        weights = (jnp.exp(scores - highest[:, None]) / totals[:, None]).astype(jnp.bfloat16)
        summed = summed + lax.dot_general(
            pieces[0], weights, (((1,), (1,)), ((), ())), preferred_element_type=jnp.float32
        )
        return (summed, None)

    start = jnp.zeros((targets.shape[0], sources.shape[1]), jnp.float32)
    summed, unused = lax.scan(barycentre_advance, start, (tiles, pot_tiles))
    return summed


def neighbours(own_block):
    gathered = lax.all_gather(own_block, "dom", axis=1, tiled=True)
    next_all = passed_along(gathered, "tm", -1)
    prev_all = passed_along(gathered, "tm", 1)
    return (next_all, prev_all)


def potentials_from(values, offset):
    gathered = lax.all_gather(values, "dom", axis=0, tiled=True)
    return passed_along(gathered, "tm", offset)


def per_device(particles, noise):
    points = particles[0]
    rounded = points.astype(jnp.bfloat16)
    next_all, prev_all = neighbours(rounded)
    time_index = lax.axis_index("tm")
    last_time = lax.axis_size("tm") - 1
    next_pot = -0.5 * jnp.sum(jnp.square(next_all.astype(jnp.float32)), axis=0)
    for sweep_index in range(SWEEPS):
        if sweep_index > 0:
            next_pot = potentials_from(target_pot, -1)
        source_pot, unused_high, unused_totals = update(rounded, next_all, next_pot)
        prev_pot = potentials_from(source_pot, 1)
        target_pot, prev_high, prev_totals = update(rounded, prev_all, prev_pot)
    next_pot = potentials_from(target_pot, -1)
    next_tiles, next_pot_tiles = col_tiles(next_all, next_pot)
    next_high, next_totals = log_totals(rounded, next_tiles, next_pot_tiles)
    bary_next = barycentre(rounded, next_all, next_pot, next_high, next_totals)
    bary_prev = barycentre(rounded, prev_all, prev_pot, prev_high, prev_totals)
    pull_next = jnp.where(time_index < last_time, points - bary_next, 0.0)
    pull_prev = jnp.where(time_index > 0, points - bary_prev, 0.0)
    advanced = points - STEP * (pull_next + pull_prev) + math.sqrt(2.0 * STEP * TEMP) * noise[0]
    return advanced[None]


def solution(mesh):
    in_specs = (P("tm", None, "dom"), P("tm", None, "dom"))
    out_specs = P("tm", None, "dom")
    return jax.shard_map(
        per_device, mesh=mesh, in_specs=in_specs, out_specs=out_specs, check_vma=False
    )
```

profile of v0, /device:TPU:1, one launch (start us, length us, event | category | flops | bytes accessed | tf_op | source)
XLA Modules:
  0.0 191.0 jit_solution(3282749936282625119)
XLA Ops:
  0.0 0.9 bitcast_convert_fusion
  0.9 26.9 %all_gather.15 = bf16[64,4096]{1,0:T(8,128)(2,1)S(1)} all-gather(bf16[64,512]{1,0:T(8,128)(2,1)S(1)} %bitcast_convert_fusion), channel_id=1, replica_groups=mesh['tm'=4,'dom'=8] {'dom'}, dimensions={1}, use_global_device_ids=true | all-gather | bytes 589824 | tf_op jit(solution)/shard_map/all_gather | solution.py:79
  27.9 8.0 %collective-permute-start = (bf16[64,4096]{1,0:T(8,128)(2,1)S(1)}, bf16[64,4096]{1,0:T(8,128)(2,1)S(1)}, u32[]{:S(2)}, u32[]{:S(2)}) collective-permute-start(bf16[64,4096]{1,0:T(8,128)(2,1)S(1)} %all_gather.15), channel_id=1, source_target_pairs={{8,0},{16,8},{24,16},{9,1},{17,9},{25,17},{10,2},{18,10},{26,18},{... | collective-permute-start | bytes 1572872 | tf_op jit(solution)/shard_map/ppermute | solution.py:19
  35.9 3.0 %collective-permute-start.1 = (bf16[64,4096]{1,0:T(8,128)(2,1)S(1)}, bf16[64,4096]{1,0:T(8,128)(2,1)}, u32[]{:S(2)}, u32[]{:S(2)}) collective-permute-start(bf16[64,4096]{1,0:T(8,128)(2,1)S(1)} %all_gather.15), channel_id=1, source_target_pairs={{0,8},{8,16},{16,24},{1,9},{9,17},{17,25},{2,10},{10,18},{18,26},{... | collective-permute-start | bytes 1572872 | tf_op jit(solution)/shard_map/ppermute | solution.py:19
  39.0 4.9 %collective-permute-done = bf16[64,4096]{1,0:T(8,128)(2,1)S(1)} collective-permute-done((bf16[64,4096]{1,0:T(8,128)(2,1)S(1)}, bf16[64,4096]{1,0:T(8,128)(2,1)S(1)}, u32[]{:S(2)}, u32[]{:S(2)}) %collective-permute-start) | collective-permute-done | bytes 524320 | tf_op jit(solution)/shard_map/ppermute | solution.py:19
  44.1 4.3 %while.87 = (s32[]{:T(128)}, f32[512]{0:T(512)S(1)}, f32[512]{0:T(512)S(1)}, bf16[4,64,1024]{2,1,0:T(8,128)(2,1)S(1)}, bf16[64,512]{1,0:T(8,128)(2,1)S(1)}, /*index=5*/f32[4,1024]{1,0:T(4,128)S(1)}, s32[]{:T(128)}, s32[]{:T(128)}) while((s32[]{:T(128)}, f32[512]{0:T(512)S(1)}, f32[512]{0:T(512)S(1)}, ...), condition=%wide.region_4.5_spmd.clone, body=%wide.region_1.4_spmd.clone.sunk | while | flops 70781440 | bytes 4434024 | solution.py:51
  44.6 0.5 exponential_reduce_fusion.10
  45.2 0.5 fusion.92
  45.7 0.5 exponential_reduce_fusion.10
  46.8 0.5 exponential_reduce_fusion.10
  48.4 21.5 %all-gather = f32[8,1,512]{2,1,0:T(1,128)S(1)} all-gather(f32[1,1,512]{2,1,0:T(1,128)S(1)} %bitcast.159), channel_id=1, replica_groups=mesh['tm'=4,'dom'=8] {'dom'}, dimensions={0}, use_global_device_ids=true | all-gather | bytes 18432 | tf_op jit(solution)/shard_map/all_gather | solution.py:86
  69.9 6.3 %collective-permute-start.2 = (f32[4096]{0:T(1024)S(1)}, f32[4096]{0:T(1024)S(1)}, u32[]{:S(2)}, u32[]{:S(2)}) collective-permute-start(f32[4096]{0:T(1024)S(1)} %bitcast.157), channel_id=1, source_target_pairs={{0,8},{8,16},{16,24},{1,9},{9,17},{17,25},{2,10},{10,18},{18,26},{... | collective-permute-start | bytes 49160 | tf_op jit(solution)/shard_map/ppermute | solution.py:19
  76.3 1.1 copy.11
  77.4 4.3 %while.88 = (s32[]{:T(128)}, f32[512]{0:T(512)S(1)}, f32[512]{0:T(512)S(1)}, bf16[4,64,1024]{2,1,0:T(8,128)(2,1)S(1)}, bf16[64,512]{1,0:T(8,128)(2,1)S(1)}, /*index=5*/f32[4,1024]{1,0:T(4,128)S(1)}, s32[]{:T(128)}, s32[]{:T(128)}) while((s32[]{:T(128)}, f32[512]{0:T(512)S(1)}, f32[512]{0:T(512)S(1)}, ...), condition=%wide.region_8.9_spmd.clone, body=%wide.region_5.8_spmd.clone.sunk | while | flops 70781440 | bytes 4434024 | solution.py:51
  77.9 0.5 exponential_reduce_fusion.11
  79.0 0.5 exponential_reduce_fusion.11
  80.1 0.5 exponential_reduce_fusion.11
  81.1 0.5 exponential_reduce_fusion.11
  81.7 21.5 %all-gather.1 = f32[8,1,512]{2,1,0:T(1,128)S(1)} all-gather(f32[1,1,512]{2,1,0:T(1,128)S(1)} %bitcast.160), channel_id=1, replica_groups=mesh['tm'=4,'dom'=8] {'dom'}, dimensions={0}, use_global_device_ids=true | all-gather | bytes 18432 | tf_op jit(solution)/shard_map/all_gather | solution.py:86
  103.2 2.6 %collective-permute-start.3 = (f32[4096]{0:T(1024)S(1)}, f32[4096]{0:T(1024)S(1)}, u32[]{:S(2)}, u32[]{:S(2)}) collective-permute-start(f32[4096]{0:T(1024)S(1)} %bitcast.158), channel_id=1, source_target_pairs={{8,0},{16,8},{24,16},{9,1},{17,9},{25,17},{10,2},{18,10},{26,18},{... | collective-permute-start | bytes 49160 | tf_op jit(solution)/shard_map/ppermute | solution.py:19
  105.8 7.3 %collective-permute-done.3 = f32[4096]{0:T(1024)S(1)} collective-permute-done((f32[4096]{0:T(1024)S(1)}, f32[4096]{0:T(1024)S(1)}, u32[]{:S(2)}, u32[]{:S(2)}) %collective-permute-start.3) | collective-permute-done | bytes 16416 | tf_op jit(solution)/shard_map/ppermute | solution.py:19
  113.1 4.3 %while.89 = (s32[]{:T(128)}, f32[512]{0:T(512)S(1)}, f32[512]{0:T(512)S(1)}, bf16[4,64,1024]{2,1,0:T(8,128)(2,1)S(1)}, bf16[64,512]{1,0:T(8,128)(2,1)S(1)}, /*index=5*/f32[4,1024]{1,0:T(4,128)S(1)}, s32[]{:T(128)}, s32[]{:T(128)}) while((s32[]{:T(128)}, f32[512]{0:T(512)S(1)}, f32[512]{0:T(512)S(1)}, ...), condition=%wide.region_12.13_spmd.clone, body=%wide.region_9.12_spmd.clone.sunk | while | flops 70781440 | bytes 4434024 | solution.py:51
  113.7 0.5 exponential_reduce_fusion.12
  114.8 0.5 exponential_reduce_fusion.12
  115.8 0.5 exponential_reduce_fusion.12
  116.9 0.5 exponential_reduce_fusion.12
  117.5 21.5 %all-gather.2 = f32[8,1,512]{2,1,0:T(1,128)S(1)} all-gather(f32[1,1,512]{2,1,0:T(1,128)S(1)} %bitcast.161), channel_id=1, replica_groups=mesh['tm'=4,'dom'=8] {'dom'}, dimensions={0}, use_global_device_ids=true | all-gather | bytes 18432 | tf_op jit(solution)/shard_map/all_gather | solution.py:86
  139.0 6.5 %collective-permute-start.4 = (f32[4096]{0:T(1024)S(1)}, f32[4096]{0:T(1024)S(1)}, u32[]{:S(2)}, u32[]{:S(2)}) collective-permute-start(f32[4096]{0:T(1024)S(1)} %bitcast.156), channel_id=1, source_target_pairs={{0,8},{8,16},{16,24},{1,9},{9,17},{17,25},{2,10},{10,18},{18,26},{... | collective-permute-start | bytes 49160 | tf_op jit(solution)/shard_map/ppermute | solution.py:19
  145.6 0.8 collective-permute-done.4
  146.4 4.3 %while.90 = (s32[]{:T(128)}, f32[512]{0:T(512)S(1)}, f32[512]{0:T(512)S(1)}, bf16[4,64,1024]{2,1,0:T(8,128)(2,1)S(1)}, bf16[64,512]{1,0:T(8,128)(2,1)S(1)}, /*index=5*/f32[4,1024]{1,0:T(4,128)S(1)}, s32[]{:T(128)}, s32[]{:T(128)}) while((s32[]{:T(128)}, f32[512]{0:T(512)S(1)}, f32[512]{0:T(512)S(1)}, ...), condition=%wide.region_16.17_spmd.clone, body=%wide.region_13.16_spmd.clone.sunk | while | flops 70781440 | bytes 4434024 | solution.py:51
  146.9 0.5 exponential_reduce_fusion.13
  148.0 0.5 exponential_reduce_fusion.13
  150.6 21.5 %all-gather.3 = f32[8,1,512]{2,1,0:T(1,128)S(1)} all-gather(f32[1,1,512]{2,1,0:T(1,128)S(1)} %bitcast.162), channel_id=1, replica_groups=mesh['tm'=4,'dom'=8] {'dom'}, dimensions={0}, use_global_device_ids=true | all-gather | bytes 18432 | tf_op jit(solution)/shard_map/all_gather | solution.py:86
  172.2 2.4 %collective-permute-start.5 = (f32[4096]{0:T(1024)S(1)}, f32[4096]{0:T(1024)S(1)}, u32[]{:S(2)}, u32[]{:S(2)}) collective-permute-start(f32[4096]{0:T(1024)S(1)} %bitcast.155), channel_id=1, source_target_pairs={{8,0},{16,8},{24,16},{9,1},{17,9},{25,17},{10,2},{18,10},{26,18},{... | collective-permute-start | bytes 49160 | tf_op jit(solution)/shard_map/ppermute | solution.py:19
  174.5 3.5 %while.93 = (s32[]{:T(128)}, f32[64,512]{1,0:T(8,128)S(1)}, bf16[4,64,1024]{2,1,0:T(8,128)(2,1)S(1)}, bf16[64,512]{1,0:T(8,128)(2,1)S(1)}, f32[4,1024]{1,0:T(4,1...) while((s32[]{:T(128)}, f32[64,512]{1,0:T(8,128)S(1)}, ...), condition=%wide.region_24.25_spmd.clone, body=%wide.region_23.24_spmd.clone.sunk | while | flops 136904704 | bytes 607339 | solution.py:74
  174.6 0.8 fusion.113
  175.4 0.8 fusion.113
  176.3 0.8 fusion.113
  177.2 0.8 fusion.113
  178.0 4.3 %collective-permute-done.5 = f32[4096]{0:T(1024)S(1)} collective-permute-done((f32[4096]{0:T(1024)S(1)}, f32[4096]{0:T(1024)S(1)}, u32[]{:S(2)}, u32[]{:S(2)}) %collective-permute-start.5) | collective-permute-done | bytes 16416 | tf_op jit(solution)/shard_map/ppermute | solution.py:19
  182.4 4.3 %while.91 = (s32[]{:T(128)}, f32[512]{0:T(512)S(1)}, f32[512]{0:T(512)S(1)}, bf16[4,64,1024]{2,1,0:T(8,128)(2,1)S(1)}, bf16[64,512]{1,0:T(8,128)(2,1)S(1)}, /*index=5*/f32[4,1024]{1,0:T(4,128)S(1)}, s32[]{:T(128)}, s32[]{:T(128)}) while((s32[]{:T(128)}, f32[512]{0:T(512)S(1)}, f32[512]{0:T(512)S(1)}, ...), condition=%wide.region_20.21_spmd.clone, body=%wide.region_17.20_spmd.clone.sunk | while | flops 70781440 | bytes 4434024 | solution.py:51
  183.5 0.5 fusion.104
  186.7 3.5 %while.92 = (s32[]{:T(128)}, f32[64,512]{1,0:T(8,128)S(1)}, bf16[4,64,1024]{2,1,0:T(8,128)(2,1)S(1)}, bf16[64,512]{1,0:T(8,128)(2,1)S(1)}, f32[4,1024]{1,0:T(4,1...) while((s32[]{:T(128)}, f32[64,512]{1,0:T(8,128)S(1)}, ...), condition=%wide.region_22.23_spmd.clone, body=%wide.region_21.22_spmd.clone.sunk | while | flops 136904704 | bytes 607339 | solution.py:74
  186.7 0.8 fusion.109
  187.6 0.8 fusion.109
  188.5 0.8 fusion.109
  189.4 0.8 fusion.109
  190.2 0.7 fusion.56
  (143 shorter events, 13.4 us)
Async XLA Ops:
  27.9 16.0 %collective-permute-start = (bf16[64,4096]{1,0:T(8,128)(2,1)S(1)}, bf16[64,4096]{1,0:T(8,128)(2,1)S(1)}, u32[]{:S(2)}, u32[]{:S(2)}) collective-permute-start(bf16[64,4096]{1,0:T(8,128)(2,1)S(1)} %all_gather.15), channel_id=1, source_target_pairs={{8,0},{16,8},{24,16},{9,1},{17,9},{25,17},{10,2},{18,10},{26,18},{... | collective-permute-start | bytes 1572872 | tf_op jit(solution)/shard_map/ppermute | solution.py:19
  35.9 40.4 %collective-permute-start.1 = (bf16[64,4096]{1,0:T(8,128)(2,1)S(1)}, bf16[64,4096]{1,0:T(8,128)(2,1)}, u32[]{:S(2)}, u32[]{:S(2)}) collective-permute-start(bf16[64,4096]{1,0:T(8,128)(2,1)S(1)} %all_gather.15), channel_id=1, source_target_pairs={{0,8},{8,16},{16,24},{1,9},{9,17},{17,25},{2,10},{10,18},{18,26},{... | collective-permute-start | bytes 1572872 | tf_op jit(solution)/shard_map/ppermute | solution.py:19
  69.9 7.5 %collective-permute-start.2 = (f32[4096]{0:T(1024)S(1)}, f32[4096]{0:T(1024)S(1)}, u32[]{:S(2)}, u32[]{:S(2)}) collective-permute-start(f32[4096]{0:T(1024)S(1)} %bitcast.157), channel_id=1, source_target_pairs={{0,8},{8,16},{16,24},{1,9},{9,17},{17,25},{2,10},{10,18},{18,26},{... | collective-permute-start | bytes 49160 | tf_op jit(solution)/shard_map/ppermute | solution.py:19
  103.2 9.9 %collective-permute-start.3 = (f32[4096]{0:T(1024)S(1)}, f32[4096]{0:T(1024)S(1)}, u32[]{:S(2)}, u32[]{:S(2)}) collective-permute-start(f32[4096]{0:T(1024)S(1)} %bitcast.158), channel_id=1, source_target_pairs={{8,0},{16,8},{24,16},{9,1},{17,9},{25,17},{10,2},{18,10},{26,18},{... | collective-permute-start | bytes 49160 | tf_op jit(solution)/shard_map/ppermute | solution.py:19
  139.0 7.4 %collective-permute-start.4 = (f32[4096]{0:T(1024)S(1)}, f32[4096]{0:T(1024)S(1)}, u32[]{:S(2)}, u32[]{:S(2)}) collective-permute-start(f32[4096]{0:T(1024)S(1)} %bitcast.156), channel_id=1, source_target_pairs={{0,8},{8,16},{16,24},{1,9},{9,17},{17,25},{2,10},{10,18},{18,26},{... | collective-permute-start | bytes 49160 | tf_op jit(solution)/shard_map/ppermute | solution.py:19
  172.2 10.2 %collective-permute-start.5 = (f32[4096]{0:T(1024)S(1)}, f32[4096]{0:T(1024)S(1)}, u32[]{:S(2)}, u32[]{:S(2)}) collective-permute-start(f32[4096]{0:T(1024)S(1)} %bitcast.155), channel_id=1, source_target_pairs={{8,0},{16,8},{24,16},{9,1},{17,9},{25,17},{10,2},{18,10},{26,18},{... | collective-permute-start | bytes 49160 | tf_op jit(solution)/shard_map/ppermute | solution.py:19
  186.7 3.5 %copy-start = (f32[1,64,512]{2,1,0:T(8,128)S(1)}, f32[1,64,512]{2,1,0:T(8,128)}, u32[]{:S(2)}) copy-start(f32[1,64,512]{2,1,0:T(8,128)} %param.16) | copy-start | bytes 393220
  186.7 3.5 %copy-start.1 = (f32[1,64,512]{2,1,0:T(8,128)S(1)}, f32[1,64,512]{2,1,0:T(8,128)}, u32[]{:S(2)}) copy-start(f32[1,64,512]{2,1,0:T(8,128)} %param.17) | copy-start | bytes 393220
where the time goes:
time: 191 us
  blocking collectives  113 us (59%)
  starting transfers between devices  28.8 us (15%)
  waiting for transfers between devices  17.4 us (9%)
  matrix products  16.5 us (9%)
  other arithmetic  12.2 us (6%)
    all_gather x4, blocking collectives, potentials_from(): gathered = lax.all_gather(values, 'dom', axis=0, tiled=True)  86.1 us
    ppermute x6, starting transfers between devices, passed_along(): lax.ppermute(value, axis, [(source, source + steps) for source in range(l...  28.8 us
    all_gather x1, blocking collectives, neighbours(): gathered = lax.all_gather(own_block, 'dom', axis=1, tiled=True)  26.9 us
    ppermute x6, waiting for transfers between devices, passed_along(): lax.ppermute(value, axis, [(source, source + steps) for source in range(l...  17.4 us
    reduce_sum x20, other arithmetic, log_advance(): jnp.sum(jnp.exp(scores - merged[:, None]), axis=1)  9.89 us
    dot_general x20, matrix products, tile_scores(): lax.dot_general(sources, target_tile, (((0,), (0,)), ((), ())), preferred...  9.87 us
    dot_general x8, matrix products, barycentre_advance(): lax.dot_general(pieces[0], weights, (((1,), (1,)), ((), ())), preferred_e...  6.65 us
  transfers between devices with their start and end apart: 6, of which 4 were waited for; matrix products, arithmetic and copies ran while one was open for 5% of the time, Pallas kernels for 0%

commit v1 on v0

v1 whole, which is shorter than its diff:
```python
import functools
import math

import jax
import jax.numpy as jnp
from jax import lax
from jax.experimental import pallas as pl
from jax.experimental.pallas import tpu as pltpu
from jax.sharding import PartitionSpec as P

SWEEPS = 2
EPS = 4.0
STEP = 0.5
TEMP = 0.05
MESH = pl.DeviceIdType.MESH
EXTRA = 16
CHUNK = 256


def crossed(me, i, n):
    total = 0
    bit = 1
    while bit < n:
        mine, its = (me // bit) % 2, (i // bit) % 2
        total = total + bit * (mine + its - 2 * mine * its)
        bit *= 2
    return total


def kernel(
    times, n, points_ref, pull_ref,
    own, nxt, prv, npot, ppot, spot, tpot, xa, ya, m_ref, l_ref, acc,
    own_s, own_r, nxt_s, nxt_r, prv_s, prv_r, npot_s, npot_r, ppot_s, ppot_r,
):
    t = lax.axis_index("tm")
    me = lax.axis_index("dom")
    dim, width = points_ref.shape
    has_next = t < times - 1
    has_prev = t > 0
    low = 2 if n > 1 else 1
    log_count = EPS * math.log(n * width)

    points = points_ref[...]
    rounded = points.astype(jnp.bfloat16)
    own[me] = rounded
    xa[pl.ds(0, dim), :] = (rounded.astype(jnp.float32) * (1.0 / EPS)).astype(jnp.bfloat16)
    rows = lax.broadcasted_iota(jnp.int32, (EXTRA, width), 0)
    xa[pl.ds(dim, EXTRA), :] = jnp.where(rows < 3, 1.0 / EPS, 0.0).astype(jnp.bfloat16)

    barrier = pltpu.get_barrier_semaphore()
    same = [i for i in range(1, n) if i % low == 0 or i == 1]
    for i in same:
        pl.semaphore_signal(barrier, inc=1, device_id=(t, crossed(me, i, n)), device_id_type=MESH)

    @pl.when(has_next)
    def _():
        for i in range(n):
            pl.semaphore_signal(barrier, inc=1, device_id=(t + 1, crossed(me, i, n)), device_id_type=MESH)

    @pl.when(has_prev)
    def _():
        for i in range(n):
            pl.semaphore_signal(barrier, inc=1, device_id=(t - 1, crossed(me, i, n)), device_id_type=MESH)

    sides = has_next.astype(jnp.int32) + has_prev.astype(jnp.int32)
    pl.semaphore_wait(barrier, len(same) + n * sides)

    def own_copy(i, block, slot):
        return pltpu.make_async_remote_copy(
            src_ref=own.at[block], dst_ref=own.at[block], send_sem=own_s.at[slot], recv_sem=own_r.at[block],
            device_id=(t, crossed(me, i, n)), device_id_type=MESH)

    def to_prev(block):
        return pltpu.make_async_remote_copy(
            src_ref=own.at[block], dst_ref=nxt.at[block], send_sem=nxt_s.at[block], recv_sem=nxt_r.at[block],
            device_id=(t - 1, me), device_id_type=MESH)

    def to_next(block):
        return pltpu.make_async_remote_copy(
            src_ref=own.at[block], dst_ref=prv.at[block], send_sem=prv_s.at[block], recv_sem=prv_r.at[block],
            device_id=(t + 1, me), device_id_type=MESH)

    for i in range(low, n, low):
        own_copy(i, me, i).start()

    def pass_on(i):
        block = crossed(me, i, n)
        if i > 0:
            own_copy(i if i % low == 0 else 1, block, 0).wait_recv()
        if i % low == 0 and low > 1:
            own_copy(1, block, i + 1).start()

        @pl.when(has_prev)
        def _():
            to_prev(block).start()

        @pl.when(has_next)
        def _():
            to_next(block).start()

    order = [0]
    for i in range(low, n, low):
        order += [i, i - low + 1] if low > 1 else [i]
    if low > 1:
        order.append(n - 1)
    for i in order:
        pass_on(i)

    def extend(block_ref, pot):
        ya[pl.ds(0, dim), :] = block_ref[...]
        high = pot.astype(jnp.bfloat16).astype(jnp.float32)
        rest = pot - high
        middle = rest.astype(jnp.bfloat16).astype(jnp.float32)
        least = rest - middle
        pieces = jnp.where(rows == 0, high, jnp.where(rows == 1, middle, jnp.where(rows == 2, least, 0.0)))
        ya[pl.ds(dim, EXTRA), :] = pieces.astype(jnp.bfloat16)

    def scores_of(start):
        return lax.dot_general(
            ya[:, pl.ds(start, CHUNK)], xa[...], (((0,), (0,)), ((), ())), preferred_element_type=jnp.float32)

    def reset():
        m_ref[...] = jnp.full_like(m_ref, -jnp.inf)
        l_ref[...] = jnp.zeros_like(l_ref)

    def log_block():
        for start in range(0, width, CHUNK):
            scores = scores_of(start)
            m_old = m_ref[...]
            m_new = jnp.maximum(m_old, jnp.max(scores, axis=0, keepdims=True))
            l_ref[...] = l_ref[...] * jnp.exp(m_old - m_new) + jnp.sum(
                jnp.exp(scores - m_new), axis=0, keepdims=True)
            m_ref[...] = m_new

    def mean_block(block_ref, total):
        for start in range(0, width, CHUNK):
            scores = scores_of(start)
            m_old = m_ref[...]
            m_new = jnp.maximum(m_old, jnp.max(scores, axis=0, keepdims=True))
            scale = jnp.exp(m_old - m_new)
            weights = jnp.exp(scores - m_new)
            l_ref[...] = l_ref[...] * scale + jnp.sum(weights, axis=0, keepdims=True)
            m_ref[...] = m_new
            total[...] = total[...] * scale + lax.dot_general(
                block_ref[:, pl.ds(start, CHUNK)], weights.astype(jnp.bfloat16), (((1,), (0,)), ((), ())),
                preferred_element_type=jnp.float32)

    def result():
        return -EPS * (m_ref[...] + jnp.log(l_ref[...])) + log_count

    def spot_copy(sweep, i):
        return pltpu.make_async_remote_copy(
            src_ref=spot.at[sweep], dst_ref=ppot.at[sweep, me], send_sem=ppot_s.at[sweep, i],
            recv_sem=ppot_r.at[sweep, me], device_id=(t + 1, crossed(me, i, n)), device_id_type=MESH)

    def tpot_copy(sweep, i):
        return pltpu.make_async_remote_copy(
            src_ref=tpot.at[sweep], dst_ref=npot.at[sweep, me], send_sem=npot_s.at[sweep, i],
            recv_sem=npot_r.at[sweep, me], device_id=(t - 1, crossed(me, i, n)), device_id_type=MESH)

    def await_ppot(sweep, block):
        pltpu.make_async_remote_copy(
            src_ref=spot.at[sweep], dst_ref=ppot.at[sweep, block], send_sem=ppot_s.at[sweep, 0],
            recv_sem=ppot_r.at[sweep, block], device_id=(t - 1, block), device_id_type=MESH).wait_recv()

    def await_npot(sweep, block):
        pltpu.make_async_remote_copy(
            src_ref=tpot.at[sweep], dst_ref=npot.at[sweep, block], send_sem=npot_s.at[sweep, 0],
            recv_sem=npot_r.at[sweep, block], device_id=(t + 1, block), device_id_type=MESH).wait_recv()

    def source_pass(sweep):
        @pl.when(has_next)
        def _():
            reset()

            @pl.loop(0, n)
            def _(i):
                block = crossed(me, i, n)
                if sweep == 0:
                    to_prev_like(block, nxt, nxt_s, nxt_r, t + 1).wait_recv()
                    extend(nxt.at[block], -0.5 * jnp.sum(
                        jnp.square(nxt[block].astype(jnp.float32)), axis=0, keepdims=True))
                else:
                    await_npot(sweep - 1, block)
                    extend(nxt.at[block], npot[sweep - 1, block])
                log_block()

            spot[sweep] = result()
            for i in reversed(range(n)):
                spot_copy(sweep, i).start()

    def to_prev_like(block, slots, sends, recvs, where):
        return pltpu.make_async_remote_copy(
            src_ref=own.at[block], dst_ref=slots.at[block], send_sem=sends.at[block], recv_sem=recvs.at[block],
            device_id=(where, me), device_id_type=MESH)

    def target_pass(sweep):
        @pl.when(has_prev)
        def _():
            reset()
            if sweep == SWEEPS - 1:
                acc[...] = jnp.zeros_like(acc)

            @pl.loop(0, n)
            def _(i):
                block = crossed(me, i, n)
                if sweep == 0:
                    to_prev_like(block, prv, prv_s, prv_r, t - 1).wait_recv()
                await_ppot(sweep, block)
                extend(prv.at[block], ppot[sweep, block])
                if sweep == SWEEPS - 1:
                    mean_block(prv.at[block], acc)
                else:
                    log_block()

            tpot[sweep] = result()
            for i in reversed(range(n)):
                tpot_copy(sweep, i).start()

    for sweep in range(SWEEPS):
        source_pass(sweep)
        target_pass(sweep)

    @pl.when(has_prev)
    def _():
        pull_ref[...] = points_ref[...] - acc[...] / l_ref[...]

    @pl.when(jnp.logical_not(has_prev))
    def _():
        pull_ref[...] = jnp.zeros_like(pull_ref)

    @pl.when(has_next)
    def _():
        reset()
        acc[...] = jnp.zeros_like(acc)

        @pl.loop(0, n)
        def _(i):
            block = crossed(me, i, n)
            await_npot(SWEEPS - 1, block)
            extend(nxt.at[block], npot[SWEEPS - 1, block])
            mean_block(nxt.at[block], acc)

        pull_ref[...] = pull_ref[...] + (points_ref[...] - acc[...] / l_ref[...])

    for i in range(low, n, low):
        own_copy(i, me, i).wait_send()
    if low > 1:
        for i in range(0, n, low):
            own_copy(1, crossed(me, i, n), i + 1).wait_send()

    @pl.when(has_prev)
    def _():
        for i in range(n):
            to_prev(i).wait_send()
            for sweep in range(SWEEPS):
                tpot_copy(sweep, i).wait_send()

    @pl.when(has_next)
    def _():
        for i in range(n):
            to_next(i).wait_send()
            for sweep in range(SWEEPS):
                spot_copy(sweep, i).wait_send()


def per_device(times, n, particles, noise):
    points = particles[0]
    dim, width = points.shape
    dma = pltpu.SemaphoreType.DMA
    row = (1, width)
    pull = pl.pallas_call(
        functools.partial(kernel, times, n),
        out_shape=jax.ShapeDtypeStruct((dim, width), jnp.float32),
        in_specs=[pl.BlockSpec(memory_space=pltpu.VMEM)],
        out_specs=pl.BlockSpec(memory_space=pltpu.VMEM),
        scratch_shapes=[
            pltpu.VMEM((n, dim, width), jnp.bfloat16),
            pltpu.VMEM((n, dim, width), jnp.bfloat16),
            pltpu.VMEM((n, dim, width), jnp.bfloat16),
            pltpu.VMEM((SWEEPS, n) + row, jnp.float32),
            pltpu.VMEM((SWEEPS, n) + row, jnp.float32),
            pltpu.VMEM((SWEEPS,) + row, jnp.float32),
            pltpu.VMEM((SWEEPS,) + row, jnp.float32),
            pltpu.VMEM((dim + EXTRA, width), jnp.bfloat16),
            pltpu.VMEM((dim + EXTRA, width), jnp.bfloat16),
            pltpu.VMEM(row, jnp.float32),
            pltpu.VMEM(row, jnp.float32),
            pltpu.VMEM((dim, width), jnp.float32),
            dma((n,)), dma((n,)), dma((n,)), dma((n,)), dma((n,)), dma((n,)),
            dma((SWEEPS, n)), dma((SWEEPS, n)), dma((SWEEPS, n)), dma((SWEEPS, n)),
        ],
        compiler_params=pltpu.CompilerParams(collective_id=0, has_side_effects=True),
    )(points)
    advanced = points - STEP * pull + math.sqrt(2.0 * STEP * TEMP) * noise[0]
    return advanced[None]


def solution(mesh):
    times, n = mesh.shape["tm"], mesh.shape["dom"]
    assert n & (n - 1) == 0
    spec = P("tm", None, "dom")
    return jax.shard_map(
        functools.partial(per_device, times, n), mesh=mesh, in_specs=(spec, spec), out_specs=spec, check_vma=False)
```

time: 191 us -> 56.3 us (0.29)
  blocking collectives: 113 us -> 0 us
  Pallas kernels: 0 us -> 54.6 us
  starting transfers between devices: 28.8 us -> 0 us
  waiting for transfers between devices: 17.4 us -> 0 us
  matrix products: 16.5 us -> 0 us
  other arithmetic: 12.2 us -> 1.59 us
    all_gather x5 -> x0, blocking collectives: 113 us -> none  [the longest x4 86.1 us: potentials_from(): gathered = lax.all_gather(values, 'dom', axis=0, tiled=True)]
    pallas_call x0 -> x1, Pallas kernels: none -> 54.6 us  [per_device(): pl.pallas_call(functools.partial(kernel, times, n), out_shape=jax.ShapeDt...]
    ppermute x6 -> x0, starting transfers between devices: 28.8 us -> none  [passed_along(): lax.ppermute(value, axis, [(source, source + steps) for source in range(l...]
    ppermute x6 -> x0, waiting for transfers between devices: 17.4 us -> none  [passed_along(): lax.ppermute(value, axis, [(source, source + steps) for source in range(l...]
    dot_general x28 -> x0, matrix products: 16.5 us -> none  [the longest x20 9.87 us: tile_scores(): lax.dot_general(sources, target_tile, (((0,), (0,)), ((), ())), preferred...]
    reduce_sum x21 -> x0, other arithmetic: 10 us -> none  [the longest x20 9.89 us: log_advance(): jnp.sum(jnp.exp(scores - merged[:, None]), axis=1)]
  transfers between devices with their start and end apart: 6 -> 0, of which waited for: 4 -> 0; matrix products, arithmetic and copies ran while one was open for 5% -> 0% of each run, Pallas kernels for 0% -> 0%
where the time goes in v1:
time: 56.3 us; the launch traced here: 56.2 us
  Pallas kernels  54.6 us (97%)
  other arithmetic  1.59 us (3%)
    pallas_call x1, Pallas kernels, per_device(): pl.pallas_call(functools.partial(kernel, times, n), out_shape=jax.ShapeDt...  54.6 us
    broadcast_in_dim x1, other arithmetic, per_device(): return advanced[None]  1.59 us

profile of v1, /device:TPU:1, one launch (start us, length us, event | category | flops | bytes accessed | tf_op | source)
XLA Modules:
  0.0 56.2 jit_solution(2874595448655983401)
XLA Ops:
  0.0 0.0 copy-start
  0.0 0.0 copy-start.1
  0.0 54.6 %shard_map.28 = f32[64,512]{1,0:T(8,128)} custom-call(f32[64,512]{1,0:T(8,128)} %bitcast.8), custom_call_target="tpu_custom_call" | custom-call | tf_op jit(solution)/shard_map/pallas_call | solution.py:272
  54.6 0.0 copy-done
  54.6 0.0 copy-done.1
  54.6 1.6 %fusion = f32[1,64,512]{2,1,0:T(8,128)} fusion(f32[1,64,512]{2,1,0:T(8,128)S(1)} %copy-done.1, f32[64,512]{1,0:T(8,128)} %shard_map.28, f32[1,64,512]{2,1,0:T(8,128)S(1)} %copy-done), kind=kLoop, calls=%fused_computation.1 | loop fusion | flops 131072 | bytes 524288 | tf_op jit(solution)/shard_map/broadcast_in_dim | solution.py:296
Async XLA Ops:
  0.0 54.6 %copy-start = (f32[1,64,512]{2,1,0:T(8,128)S(1)}, f32[1,64,512]{2,1,0:T(8,128)}, u32[]{:S(2)}) copy-start(f32[1,64,512]{2,1,0:T(8,128)} %param.2) | copy-start | bytes 393220
  0.0 54.6 %copy-start.1 = (f32[1,64,512]{2,1,0:T(8,128)S(1)}, f32[1,64,512]{2,1,0:T(8,128)}, u32[]{:S(2)}) copy-start(f32[1,64,512]{2,1,0:T(8,128)} %param.3) | copy-start | bytes 393220

commit v2 on v1

--- a/solution.py
+++ b/solution.py
@@ -14,7 +14,9 @@
 TEMP = 0.05
 MESH = pl.DeviceIdType.MESH
 EXTRA = 16
+PIECE = 64
 CHUNK = 256
+LAG = 2
 
 
 def crossed(me, i, n):
@@ -29,7 +31,7 @@
 
 def kernel(
     times, n, points_ref, pull_ref,
-    own, nxt, prv, npot, ppot, spot, tpot, xa, ya, m_ref, l_ref, acc,
+    own, nxt, prv, npot, ppot, spot, tpot, xa, ya, yb, sa, sb, pw, m_ref, l_ref, acc,
     own_s, own_r, nxt_s, nxt_r, prv_s, prv_r, npot_s, npot_r, ppot_s, ppot_r,
 ):
     t = lax.axis_index("tm")
@@ -54,16 +56,14 @@
 
     @pl.when(has_next)
     def _():
-        for i in range(n):
-            pl.semaphore_signal(barrier, inc=1, device_id=(t + 1, crossed(me, i, n)), device_id_type=MESH)
+        pl.semaphore_signal(barrier, inc=1, device_id=(t + 1, me), device_id_type=MESH)
 
     @pl.when(has_prev)
     def _():
-        for i in range(n):
-            pl.semaphore_signal(barrier, inc=1, device_id=(t - 1, crossed(me, i, n)), device_id_type=MESH)
+        pl.semaphore_signal(barrier, inc=1, device_id=(t - 1, me), device_id_type=MESH)
 
     sides = has_next.astype(jnp.int32) + has_prev.astype(jnp.int32)
-    pl.semaphore_wait(barrier, len(same) + n * sides)
+    pl.semaphore_wait(barrier, len(same) + sides)
 
     def own_copy(i, block, slot):
         return pltpu.make_async_remote_copy(
@@ -103,47 +103,78 @@
         order += [i, i - low + 1] if low > 1 else [i]
     if low > 1:
         order.append(n - 1)
-    for i in order:
-        pass_on(i)
-
-    def extend(block_ref, pot):
-        ya[pl.ds(0, dim), :] = block_ref[...]
+    def extend(y_ref, block_ref, pot):
+        y_ref[pl.ds(0, dim), :] = block_ref[...]
         high = pot.astype(jnp.bfloat16).astype(jnp.float32)
         rest = pot - high
         middle = rest.astype(jnp.bfloat16).astype(jnp.float32)
         least = rest - middle
         pieces = jnp.where(rows == 0, high, jnp.where(rows == 1, middle, jnp.where(rows == 2, least, 0.0)))
-        ya[pl.ds(dim, EXTRA), :] = pieces.astype(jnp.bfloat16)
-
-    def scores_of(start):
-        return lax.dot_general(
-            ya[:, pl.ds(start, CHUNK)], xa[...], (((0,), (0,)), ((), ())), preferred_element_type=jnp.float32)
+        y_ref[pl.ds(dim, EXTRA), :] = pieces.astype(jnp.bfloat16)
+
+    def folded(values, join):
+        parts = [values[r:r + 8] for r in range(0, values.shape[0], 8)]
+        while len(parts) > 1:
+            parts = [join(parts[k], parts[k + 1]) for k in range(0, len(parts) - 1, 2)] + (
+                [parts[-1]] if len(parts) % 2 else [])
+        return parts[0]
 
     def reset():
         m_ref[...] = jnp.full_like(m_ref, -jnp.inf)
         l_ref[...] = jnp.zeros_like(l_ref)
 
-    def log_block():
-        for start in range(0, width, CHUNK):
-            scores = scores_of(start)
-            m_old = m_ref[...]
-            m_new = jnp.maximum(m_old, jnp.max(scores, axis=0, keepdims=True))
-            l_ref[...] = l_ref[...] * jnp.exp(m_old - m_new) + jnp.sum(
-                jnp.exp(scores - m_new), axis=0, keepdims=True)
+    def step(y_ref, new_scores, old_scores, old_block, mean):
+        m_old = m_ref[...]
+        highest, total = None, None
+        if old_scores is not None:
+            for start in range(0, width, PIECE):
+                here = pl.ds(start, PIECE)
+                weights = jnp.exp(old_scores[here, :] - m_old)
+                part = folded(weights, jnp.add)
+                total = part if total is None else total + part
+                if mean:
+                    pw[here, :] = weights.astype(jnp.bfloat16)
+        if new_scores is not None:
+            for start in range(0, width, CHUNK):
+                here = pl.ds(start, CHUNK)
+                scores = lax.dot_general(
+                    y_ref[:, here], xa[...], (((0,), (0,)), ((), ())), preferred_element_type=jnp.float32)
+                new_scores[here, :] = scores
+                top = folded(scores, jnp.maximum)
+                highest = top if highest is None else jnp.maximum(highest, top)
+        if old_scores is not None:
+            sums = l_ref[...] + jnp.sum(total, axis=0, keepdims=True)
+            if mean:
+                for start in range(0, width, CHUNK):
+                    here = pl.ds(start, CHUNK)
+                    acc[...] += lax.dot_general(
+                        old_block[:, here], pw[here, :], (((1,), (0,)), ((), ())),
+                        preferred_element_type=jnp.float32)
+        else:
+            sums = l_ref[...]
+        if new_scores is not None:
+            m_new = jnp.maximum(m_old, jnp.max(highest, axis=0, keepdims=True))
+            scale = jnp.exp(m_old - m_new)
             m_ref[...] = m_new
-
-    def mean_block(block_ref, total):
-        for start in range(0, width, CHUNK):
-            scores = scores_of(start)
-            m_old = m_ref[...]
-            m_new = jnp.maximum(m_old, jnp.max(scores, axis=0, keepdims=True))
-            scale = jnp.exp(m_old - m_new)
-            weights = jnp.exp(scores - m_new)
-            l_ref[...] = l_ref[...] * scale + jnp.sum(weights, axis=0, keepdims=True)
-            m_ref[...] = m_new
-            total[...] = total[...] * scale + lax.dot_general(
-                block_ref[:, pl.ds(start, CHUNK)], weights.astype(jnp.bfloat16), (((1,), (0,)), ((), ())),
-                preferred_element_type=jnp.float32)
+            sums = sums * scale
+            if mean and old_scores is not None:
+                acc[...] = acc[...] * scale
+        l_ref[...] = sums
+
+    def sweep_over(prepare, slots, mean):
+        def do(i, y_ref, new, old):
+            prepare(y_ref, i)
+            step(y_ref, new, old, slots.at[crossed(me, i - 1, n)], mean)
+
+        prepare(ya, 0)
+        step(ya, sa, None, None, mean)
+        if n > 2:
+            @pl.loop(0, n // 2 - 1)
+            def _(h):
+                do(2 * h + 1, yb, sb, sa)
+                do(2 * h + 2, ya, sa, sb)
+        do(n - 1, yb, sb, sa)
+        step(None, None, sb, slots.at[crossed(me, n - 1, n)], mean)
 
     def result():
         return -EPS * (m_ref[...] + jnp.log(l_ref[...])) + log_count
@@ -168,57 +199,79 @@
             src_ref=tpot.at[sweep], dst_ref=npot.at[sweep, block], send_sem=npot_s.at[sweep, 0],
             recv_sem=npot_r.at[sweep, block], device_id=(t + 1, block), device_id_type=MESH).wait_recv()
 
+    def landed(block, slots, sends, recvs):
+        pltpu.make_async_remote_copy(
+            src_ref=own.at[block], dst_ref=slots.at[block], send_sem=sends.at[block], recv_sem=recvs.at[block],
+            device_id=(t, me), device_id_type=MESH).wait_recv()
+
+    def send_source(sweep):
+        spot[sweep] = result()
+        for i in reversed(range(n)):
+            spot_copy(sweep, i).start()
+
+    def first_prepare(y_ref, i):
+        block = crossed(me, i, n)
+        landed(block, nxt, nxt_s, nxt_r)
+        extend(y_ref, nxt.at[block], -0.5 * jnp.sum(
+            jnp.square(nxt[block].astype(jnp.float32)), axis=0, keepdims=True))
+
+    @pl.when(has_next)
+    def _():
+        reset()
+
+    def first_step(k):
+        @pl.when(has_next)
+        def _():
+            y_ref, new, old = (ya, sa, sb) if k % 2 == 0 else (yb, sb, sa)
+            first_prepare(y_ref, order[k])
+            step(y_ref, new, old if k > 0 else None, None, False)
+
+    for k in range(n):
+        pass_on(order[k])
+        if k >= LAG:
+            first_step(k - LAG)
+    for k in range(max(0, n - LAG), n):
+        first_step(k)
+
+    @pl.when(has_next)
+    def _():
+        step(None, None, sb if n % 2 == 0 else sa, None, False)
+        send_source(0)
+
     def source_pass(sweep):
+        def prepare(y_ref, i):
+            block = crossed(me, i, n)
+            await_npot(sweep - 1, block)
+            extend(y_ref, nxt.at[block], npot[sweep - 1, block])
+
         @pl.when(has_next)
         def _():
             reset()
-
-            @pl.loop(0, n)
-            def _(i):
-                block = crossed(me, i, n)
-                if sweep == 0:
-                    to_prev_like(block, nxt, nxt_s, nxt_r, t + 1).wait_recv()
-                    extend(nxt.at[block], -0.5 * jnp.sum(
-                        jnp.square(nxt[block].astype(jnp.float32)), axis=0, keepdims=True))
-                else:
-                    await_npot(sweep - 1, block)
-                    extend(nxt.at[block], npot[sweep - 1, block])
-                log_block()
-
-            spot[sweep] = result()
-            for i in reversed(range(n)):
-                spot_copy(sweep, i).start()
-
-    def to_prev_like(block, slots, sends, recvs, where):
-        return pltpu.make_async_remote_copy(
-            src_ref=own.at[block], dst_ref=slots.at[block], send_sem=sends.at[block], recv_sem=recvs.at[block],
-            device_id=(where, me), device_id_type=MESH)
+            sweep_over(prepare, nxt, False)
+            send_source(sweep)
 
     def target_pass(sweep):
+        def prepare(y_ref, i):
+            block = crossed(me, i, n)
+            if sweep == 0:
+                landed(block, prv, prv_s, prv_r)
+            await_ppot(sweep, block)
+            extend(y_ref, prv.at[block], ppot[sweep, block])
+
         @pl.when(has_prev)
         def _():
             reset()
-            if sweep == SWEEPS - 1:
+            mean = sweep == SWEEPS - 1
+            if mean:
                 acc[...] = jnp.zeros_like(acc)
-
-            @pl.loop(0, n)
-            def _(i):
-                block = crossed(me, i, n)
-                if sweep == 0:
-                    to_prev_like(block, prv, prv_s, prv_r, t - 1).wait_recv()
-                await_ppot(sweep, block)
-                extend(prv.at[block], ppot[sweep, block])
-                if sweep == SWEEPS - 1:
-                    mean_block(prv.at[block], acc)
-                else:
-                    log_block()
-
+            sweep_over(prepare, prv, mean)
             tpot[sweep] = result()
             for i in reversed(range(n)):
                 tpot_copy(sweep, i).start()
 
     for sweep in range(SWEEPS):
-        source_pass(sweep)
+        if sweep > 0:
+            source_pass(sweep)
         target_pass(sweep)
 
     @pl.when(has_prev)
@@ -234,13 +287,12 @@
         reset()
         acc[...] = jnp.zeros_like(acc)
 
-        @pl.loop(0, n)
-        def _(i):
+        def prepare(y_ref, i):
             block = crossed(me, i, n)
             await_npot(SWEEPS - 1, block)
-            extend(nxt.at[block], npot[SWEEPS - 1, block])
-            mean_block(nxt.at[block], acc)
-
+            extend(y_ref, nxt.at[block], npot[SWEEPS - 1, block])
+
+        sweep_over(prepare, nxt, True)
         pull_ref[...] = pull_ref[...] + (points_ref[...] - acc[...] / l_ref[...])
 
     for i in range(low, n, low):
@@ -284,6 +336,10 @@
             pltpu.VMEM((SWEEPS,) + row, jnp.float32),
             pltpu.VMEM((dim + EXTRA, width), jnp.bfloat16),
             pltpu.VMEM((dim + EXTRA, width), jnp.bfloat16),
+            pltpu.VMEM((dim + EXTRA, width), jnp.bfloat16),
+            pltpu.VMEM((width, width), jnp.float32),
+            pltpu.VMEM((width, width), jnp.float32),
+            pltpu.VMEM((width, width), jnp.bfloat16),
             pltpu.VMEM(row, jnp.float32),
             pltpu.VMEM(row, jnp.float32),
             pltpu.VMEM((dim, width), jnp.float32),

time: 56.3 us -> 48.6 us (0.86)
  Pallas kernels: 54.6 us -> 46.8 us
    pallas_call x1, Pallas kernels: 54.6 us -> 46.8 us  [per_device(): pl.pallas_call(functools.partial(kernel, times, n), out_shape=jax.ShapeDt...]
where the time goes in v2:
time: 48.6 us; the launch traced here: 48.5 us
  Pallas kernels  46.8 us (96%)
  other arithmetic  1.59 us (3%)
    pallas_call x1, Pallas kernels, per_device(): pl.pallas_call(functools.partial(kernel, times, n), out_shape=jax.ShapeDt...  46.8 us
    broadcast_in_dim x1, other arithmetic, per_device(): return advanced[None]  1.59 us

profile of v2, /device:TPU:1, one launch (start us, length us, event | category | flops | bytes accessed | tf_op | source)
XLA Modules:
  0.0 48.5 jit_solution(2480072139037802983)
XLA Ops:
  0.0 0.0 copy-start
  0.0 0.0 copy-start.1
  0.0 46.8 %shard_map.28 = f32[64,512]{1,0:T(8,128)} custom-call(f32[64,512]{1,0:T(8,128)} %bitcast.8), custom_call_target="tpu_custom_call" | custom-call | tf_op jit(solution)/shard_map/pallas_call | solution.py:324
  46.9 0.0 copy-done
  46.9 0.0 copy-done.1
  46.9 1.6 %fusion = f32[1,64,512]{2,1,0:T(8,128)} fusion(f32[1,64,512]{2,1,0:T(8,128)S(1)} %copy-done.1, f32[64,512]{1,0:T(8,128)} %shard_map.28, f32[1,64,512]{2,1,0:T(8,128)S(1)} %copy-done), kind=kLoop, calls=%fused_computation.1 | loop fusion | flops 131072 | bytes 524288 | tf_op jit(solution)/shard_map/broadcast_in_dim | solution.py:352
Async XLA Ops:
  0.0 46.9 %copy-start = (f32[1,64,512]{2,1,0:T(8,128)S(1)}, f32[1,64,512]{2,1,0:T(8,128)}, u32[]{:S(2)}) copy-start(f32[1,64,512]{2,1,0:T(8,128)} %param.2) | copy-start | bytes 393220
  0.0 46.9 %copy-start.1 = (f32[1,64,512]{2,1,0:T(8,128)S(1)}, f32[1,64,512]{2,1,0:T(8,128)}, u32[]{:S(2)}) copy-start(f32[1,64,512]{2,1,0:T(8,128)} %param.3) | copy-start | bytes 393220

commit v3 on v2

--- a/solution.py
+++ b/solution.py
@@ -15,8 +15,8 @@
 MESH = pl.DeviceIdType.MESH
 EXTRA = 16
 PIECE = 64
-CHUNK = 256
-LAG = 2
+CHUNK = 512
+LAG = 4
 
 
 def crossed(me, i, n):
@@ -30,7 +30,7 @@
 
 
 def kernel(
-    times, n, points_ref, pull_ref,
+    times, n, points_ref, noise_ref, out_ref,
     own, nxt, prv, npot, ppot, spot, tpot, xa, ya, yb, sa, sb, pw, m_ref, l_ref, acc,
     own_s, own_r, nxt_s, nxt_r, prv_s, prv_r, npot_s, npot_r, ppot_s, ppot_r,
 ):
@@ -276,11 +276,12 @@
 
     @pl.when(has_prev)
     def _():
-        pull_ref[...] = points_ref[...] - acc[...] / l_ref[...]
+        out_ref[...] = points_ref[...] - STEP * (points_ref[...] - acc[...] / l_ref[...]) + (
+            math.sqrt(2.0 * STEP * TEMP) * noise_ref[...])
 
     @pl.when(jnp.logical_not(has_prev))
     def _():
-        pull_ref[...] = jnp.zeros_like(pull_ref)
+        out_ref[...] = points_ref[...] + math.sqrt(2.0 * STEP * TEMP) * noise_ref[...]
 
     @pl.when(has_next)
     def _():
@@ -293,7 +294,7 @@
             extend(y_ref, nxt.at[block], npot[SWEEPS - 1, block])
 
         sweep_over(prepare, nxt, True)
-        pull_ref[...] = pull_ref[...] + (points_ref[...] - acc[...] / l_ref[...])
+        out_ref[...] = out_ref[...] - STEP * (points_ref[...] - acc[...] / l_ref[...])
 
     for i in range(low, n, low):
         own_copy(i, me, i).wait_send()
@@ -321,10 +322,10 @@
     dim, width = points.shape
     dma = pltpu.SemaphoreType.DMA
     row = (1, width)
-    pull = pl.pallas_call(
+    advanced = pl.pallas_call(
         functools.partial(kernel, times, n),
         out_shape=jax.ShapeDtypeStruct((dim, width), jnp.float32),
-        in_specs=[pl.BlockSpec(memory_space=pltpu.VMEM)],
+        in_specs=[pl.BlockSpec(memory_space=pltpu.VMEM)] * 2,
         out_specs=pl.BlockSpec(memory_space=pltpu.VMEM),
         scratch_shapes=[
             pltpu.VMEM((n, dim, width), jnp.bfloat16),
@@ -347,8 +348,7 @@
             dma((SWEEPS, n)), dma((SWEEPS, n)), dma((SWEEPS, n)), dma((SWEEPS, n)),
         ],
         compiler_params=pltpu.CompilerParams(collective_id=0, has_side_effects=True),
-    )(points)
-    advanced = points - STEP * pull + math.sqrt(2.0 * STEP * TEMP) * noise[0]
+    )(points, noise[0])
     return advanced[None]
 
 

time: 48.6 us -> 48.2 us (level)
  other arithmetic: 1.59 us -> 0 us
  local copies, waits for them, and re-layouts: 0.01 us -> 1.57 us
    broadcast_in_dim x1 -> x0, other arithmetic: 1.59 us -> none  [per_device(): return advanced[None]]
    unnamed x4 -> x1, local copies, waits for them, and re-layouts: 0.01 us -> 1.57 us
where the time goes in v3:
time: 48.2 us; the launch traced here: 48 us
  Pallas kernels  46.4 us (96%)
  local copies, waits for them, and re-layouts  1.57 us (3%)
    pallas_call x1, Pallas kernels, per_device(): pl.pallas_call(functools.partial(kernel, times, n), out_shape=jax.ShapeDt...  46.4 us
    unnamed x1, local copies, waits for them, and re-layouts  1.57 us

profile of v3, /device:TPU:1, one launch (start us, length us, event | category | flops | bytes accessed | tf_op | source)
XLA Modules:
  0.0 48.0 jit_solution(5901135697203723570)
XLA Ops:
  0.0 46.4 %shard_map.28 = f32[64,512]{1,0:T(8,128)} custom-call(f32[64,512]{1,0:T(8,128)} %bitcast.4, f32[64,512]{1,0:T(8,128)} %bitcast.5), custom_call_target="tpu_custom_call" | custom-call | tf_op jit(solution)/shard_map/pallas_call | solution.py:325
  46.5 1.6 %copy.4 = f32[1,64,512]{2,1,0:T(8,128)} copy(f32[1,64,512]{2,1,0:T(8,128)} %bitcast.3) | data formatting | bytes 262144
